TPU v7x, 32 devices: a whole 2x2x4 slice. The times are simulated.
32 devices in a mesh: dp: 8 (over y, x, core), mp: 4 (over z).
Axes of the slice: x: 2, y: 2, z: 4, core: 2. Of those that a mesh axis runs over, the one named last changes fastest.
Arguments:
- hidden_in: bfloat16 [16384, 2048], P('dp', 'mp')
- positions: int32 [16384], P('dp'), may hold values from 0 to 1023, as said below
- head_counts: int32 [4], replicated, may hold values from 4 to 6, as said below
- attention_gain: float32 [2048], P('mp'), may hold values from 0.5 to 1.5
- query_projection_weight: bfloat16 [2048, 1536], P(None, 'mp'), may hold values from -0.125 to 0.125
- key_weight: bfloat16 [2048, 320], replicated, may hold values from -0.125 to 0.125
- value_weight: bfloat16 [2048, 320], replicated, may hold values from -0.125 to 0.125
- query_gain: float32 [64], replicated, may hold values from 0.25 to 1.75
- key_gain: float32 [64], replicated, may hold values from 0.25 to 1.75
- output_weight: bfloat16 [1536, 2048], P(None, 'mp'), may hold values from -0.75 to 0.75
- feedforward_gain: float32 [2048], P('mp'), may hold values from 0.5 to 1.5
- gate_weight: bfloat16 [2048, 4096], P(None, 'mp'), may hold values from -0.125 to 0.125
- up_weight: bfloat16 [2048, 4096], P(None, 'mp'), may hold values from -0.125 to 0.125
- down_projection_weight: bfloat16 [4096, 2048], P('mp'), may hold values from -0.125 to 0.125
- cotangent: bfloat16 [16384, 2048], P('dp', 'mp'), may hold values from -6 to 6
Outputs:
- output: bfloat16 [16384, 2048], P('dp', 'mp')
- input_gradient: float32 [16384, 2048], P('dp', 'mp')
- attention_gain_gradient: float32 [2048], P('mp')
- query_weight_gradient: float32 [2048, 1536], P(None, 'mp')
- key_weight_gradient: float32 [2048, 320], replicated
- value_weight_gradient: float32 [2048, 320], replicated
- query_gain_gradient: float32 [64], replicated
- key_gain_gradient: float32 [64], replicated
- output_projection_gradient: float32 [1536, 2048], P(None, 'mp')
- feedforward_gain_gradient: float32 [2048], P('mp')
- gate_weight_gradient: float32 [2048, 4096], P(None, 'mp')
- up_weight_gradient: float32 [2048, 4096], P(None, 'mp')
- down_weight_gradient: float32 [4096, 2048], P('mp')
Inputs may be any that keep to these rules, and one draw needn't show every extreme that they name: `head_counts`: the counts sum to 20; index m's live heads follow those of lower indices; the largest count is 6 in every draw. `positions`: position ids count up by one along each sequence of 1024 tokens and restart at zero at its start and at up to three points inside it; the first sequence of all has no restart inside it.
All inputs are finite; a program needn't handle non-finite values.
Results may differ from a plain program's by a relative error of at most 0.025.
Values may be sent and summed in bfloat16 or wider, within the bound.
No kernel may reach another device: no remote copies, remote signals or barrier semaphores. Data moves between devices by JAX's collectives and lax.ppermute only.
A program may use at most 256 MiB of HBM per device.

v0:
```python
import math
import jax
import jax.numpy as jnp
from jax import lax
from jax.sharding import PartitionSpec as P

D = 2048
QH = 20
KVH = 5
HD = 64
LEN = 1024
BLK = 512
NBLK = 2
epsilon = 1e-05
rope_base = 10000.0
masked_score = -1e30


def rotary_tables(positions):
    half = HD // 2
    inverse = jnp.exp(-math.log(rope_base) * (2.0 * jnp.arange(half, dtype=jnp.float32)) / HD)
    angles = positions.astype(jnp.float32)[..., None] * inverse
    angles = jnp.concatenate([angles, angles], axis=-1)
    return (jnp.cos(angles), jnp.sin(angles))


def rotate(vectors, cosine, sine):
    half = vectors.shape[-1] // 2
    turned = jnp.concatenate([-vectors[..., half:], vectors[..., :half]], axis=-1)
    return vectors * cosine + turned * sine


def head_norm(vectors, gain):
    return vectors * lax.rsqrt(jnp.mean(vectors * vectors, axis=-1, keepdims=True) + epsilon) * gain


def inner(left_operand, right_operand):
    return lax.dot_general(
        left_operand, right_operand, (((0,), (0,)), ((), ())), preferred_element_type=jnp.float32
    )


def against(left_operand, right_operand):
    return lax.dot_general(
        left_operand, right_operand, (((1,), (1,)), ((), ())), preferred_element_type=jnp.float32
    )


def norm_forward(values, gain):
    squares = lax.psum(jnp.sum(values * values, axis=1), "mp")
    rms = lax.rsqrt(squares / D + epsilon)[:, None]
    normed = (values * rms * gain).astype(jnp.bfloat16)
    return (rms, lax.all_gather(normed, "mp", axis=1, tiled=True))


def norm_backward(values, rms, gain, normed_grad):
    weighted = normed_grad * gain
    dotted = lax.psum(jnp.sum(weighted * values, axis=1), "mp")[:, None]
    grad = weighted * rms - values * (rms * rms * rms) * dotted / D
    gain_grad = jnp.sum(normed_grad * values * rms, axis=0)
    return (grad, gain_grad)


def spread_sum(terms):
    return lax.psum_scatter(
        terms.astype(jnp.bfloat16), "mp", scatter_dimension=1, tiled=True
    ).astype(jnp.float32)


def on_device(
    hidden_in,
    positions,
    head_counts,
    attention_gain,
    query_projection_weight,
    key_weight,
    value_weight,
    query_gain,
    key_gain,
    output_weight,
    feedforward_gain,
    gate_weight,
    up_weight,
    down_projection_weight,
    cotangent,
):
    parts = lax.axis_size("mp")
    rank = lax.axis_index("mp")
    tokens = hidden_in.shape[0]
    share = hidden_in.shape[1]
    slots_here = query_projection_weight.shape[1] // HD
    seqs = tokens // LEN
    scale = 1.0 / math.sqrt(HD)
    ranks = jnp.arange(parts, dtype=jnp.int32)
    offset = jnp.sum(jnp.where(ranks < rank, head_counts, 0))
    count = jnp.sum(jnp.where(ranks == rank, head_counts, 0))
    within = jnp.arange(slots_here, dtype=jnp.int32)
    live = (within < count).astype(jnp.float32)
    groups = jnp.minimum((offset + within) // (QH // KVH), KVH - 1)
    choose = (groups[:, None] == jnp.arange(KVH, dtype=jnp.int32)[None, :]).astype(jnp.float32)
    choose_low = choose.astype(jnp.bfloat16)
    cosine, sine = rotary_tables(positions)

    def turn(raw, gain):
        heads = raw.reshape(tokens, -1, HD)
        return rotate(head_norm(heads, gain), cosine[:, None, :], sine[:, None, :])

    inputs = hidden_in.astype(jnp.float32)
    first_rms, normed_full = norm_forward(inputs, attention_gain)
    queries = jnp.dot(normed_full, query_projection_weight, preferred_element_type=jnp.float32)
    keys = jnp.dot(normed_full, key_weight, preferred_element_type=jnp.float32)
    values_low = jnp.dot(normed_full, value_weight, preferred_element_type=jnp.float32).astype(
        jnp.bfloat16
    )
    turned_queries, query_pull = jax.vjp(turn, queries, query_gain)
    turned_keys, key_pull = jax.vjp(turn, keys, key_gain)
    turned_queries = turned_queries.astype(jnp.bfloat16)
    turned_keys = turned_keys.astype(jnp.bfloat16)
    query_heads = jnp.transpose(turned_queries.reshape(seqs, LEN, slots_here, HD), (0, 2, 1, 3))
    key_heads = jnp.einsum(
        "hg,slgd->shld",
        choose_low,
        turned_keys.reshape(seqs, LEN, KVH, HD),
        preferred_element_type=jnp.float32,
    ).astype(jnp.bfloat16)
    value_heads = jnp.einsum(
        "hg,slgd->shld",
        choose_low,
        values_low.reshape(seqs, LEN, KVH, HD),
        preferred_element_type=jnp.float32,
    ).astype(jnp.bfloat16)
    query_blocks = jnp.moveaxis(query_heads.reshape(seqs, slots_here, NBLK, BLK, HD), 2, 0)
    starts = jnp.arange(NBLK, dtype=jnp.int32) * BLK
    cols = jnp.arange(LEN, dtype=jnp.int32)

    def block_scores(block, start):
        scores = (
            jnp.einsum("shid,shjd->shij", block, key_heads, preferred_element_type=jnp.float32)
            * scale
        )
        rows = start + jnp.arange(BLK, dtype=jnp.int32)
        allowed = cols[None, :] <= rows[:, None]
        return jnp.where(allowed, scores, masked_score)

    def attend_block(block_args):
        block, start = block_args
        scores = block_scores(block, start)
        peak = jnp.max(scores, axis=-1, keepdims=True)
        weights = jnp.exp(scores - peak)
        total = jnp.sum(weights, axis=-1, keepdims=True)
        probs = (weights / total).astype(jnp.bfloat16)
        result = jnp.einsum(
            "shij,shjd->shid", probs, value_heads, preferred_element_type=jnp.float32
        )
        return (result, (peak + jnp.log(total))[..., 0])

    mixed, row_totals = lax.map(attend_block, (query_blocks, starts))
    mixed = jnp.moveaxis(mixed, 0, 2).reshape(seqs, slots_here, LEN, HD).astype(jnp.bfloat16)
    mixed = mixed * live.astype(jnp.bfloat16)[None, :, None, None]
    mixed_local = jnp.transpose(mixed, (0, 2, 1, 3)).reshape(tokens, slots_here * HD)
    all_heads = lax.all_gather(mixed_local, "mp", axis=1, tiled=True)
    branch = jnp.dot(all_heads, output_weight, preferred_element_type=jnp.float32)
    middle = inputs + branch
    second_rms, second_normed_complete = norm_forward(middle, feedforward_gain)
    gate = jnp.dot(second_normed_complete, gate_weight, preferred_element_type=jnp.float32)
    up = jnp.dot(second_normed_complete, up_weight, preferred_element_type=jnp.float32)
    sigma = jax.nn.sigmoid(gate)
    swish = gate * sigma
    hidden = (swish * up).astype(jnp.bfloat16)
    down_terms = jnp.dot(hidden, down_projection_weight, preferred_element_type=jnp.float32)
    output = (
        middle
        + lax.psum_scatter(
            down_terms.astype(jnp.bfloat16), "mp", scatter_dimension=1, tiled=True
        ).astype(jnp.float32)
    ).astype(jnp.bfloat16)
    cotangent_full = lax.all_gather(cotangent, "mp", axis=1, tiled=True)
    down_grad = inner(hidden, cotangent_full)
    hidden_grad = against(cotangent_full, down_projection_weight)
    gate_grad = (hidden_grad * up * sigma * (1.0 + gate * (1.0 - sigma))).astype(jnp.bfloat16)
    up_grad = (hidden_grad * swish).astype(jnp.bfloat16)
    gate_weight_grad = inner(second_normed_complete, gate_grad)
    up_weight_grad = inner(second_normed_complete, up_grad)
    normed_two_grad = spread_sum(against(gate_grad, gate_weight) + against(up_grad, up_weight))
    middle_part, feedforward_gain_grad = norm_backward(
        middle, second_rms, feedforward_gain, normed_two_grad
    )
    middle_grad = cotangent.astype(jnp.float32) + middle_part
    branch_grad = middle_grad.astype(jnp.bfloat16)
    output_weight_grad = inner(all_heads, branch_grad)
    slot_terms = against(branch_grad, output_weight)
    mixed_grad = lax.psum_scatter(
        slot_terms.astype(jnp.bfloat16), "mp", scatter_dimension=1, tiled=True
    ).astype(jnp.float32)
    mixed_grad = (mixed_grad.reshape(tokens, slots_here, HD) * live[None, :, None]).astype(
        jnp.bfloat16
    )
    grad_heads = jnp.transpose(mixed_grad.reshape(seqs, LEN, slots_here, HD), (0, 2, 1, 3))
    grad_blocks = jnp.moveaxis(grad_heads.reshape(seqs, slots_here, NBLK, BLK, HD), 2, 0)

    def back_block(carry, block_args):
        key_total, value_total = carry
        block, grad_block, row_total, start = block_args
        scores = block_scores(block, start)
        probs = jnp.exp(scores - row_total[..., None])
        probs_low = probs.astype(jnp.bfloat16)
        prob_grad = jnp.einsum(
            "shid,shjd->shij", grad_block, value_heads, preferred_element_type=jnp.float32
        )
        delta = jnp.sum(probs * prob_grad, axis=-1, keepdims=True)
        score_grad = (probs * (prob_grad - delta)).astype(jnp.bfloat16)
        query_grad = (
            jnp.einsum("shij,shjd->shid", score_grad, key_heads, preferred_element_type=jnp.float32)
            * scale
        )
        key_total = (
            key_total
            + jnp.einsum("shij,shid->shjd", score_grad, block, preferred_element_type=jnp.float32)
            * scale
        )
        value_total = value_total + jnp.einsum(
            "shij,shid->shjd", probs_low, grad_block, preferred_element_type=jnp.float32
        )
        return ((key_total, value_total), query_grad)

    empty = jnp.zeros((seqs, slots_here, LEN, HD), jnp.float32)
    (key_slot_grad, value_slot_grad), query_block_grads = lax.scan(
        back_block, (empty, empty), (query_blocks, grad_blocks, row_totals, starts)
    )
    query_rot_grad = jnp.moveaxis(query_block_grads, 0, 2).reshape(seqs, slots_here, LEN, HD)
    query_rot_grad = jnp.transpose(query_rot_grad, (0, 2, 1, 3)).reshape(tokens, slots_here, HD)
    key_rot_grad = jnp.einsum("hg,shld->slgd", choose, key_slot_grad).reshape(tokens, KVH, HD)
    value_grad = jnp.einsum("hg,shld->slgd", choose, value_slot_grad).reshape(tokens, KVH * HD)
    query_unrotated_gradient, query_gain_part = query_pull(query_rot_grad)
    key_raw_grad, key_gain_part = key_pull(key_rot_grad)
    summed = (
        lax.psum(key_raw_grad.astype(jnp.bfloat16), "mp").astype(jnp.float32),
        lax.psum(value_grad.astype(jnp.bfloat16), "mp").astype(jnp.float32),
        lax.psum(query_gain_part.astype(jnp.bfloat16), "mp").astype(jnp.float32),
        lax.psum(key_gain_part.astype(jnp.bfloat16), "mp").astype(jnp.float32),
    )
    keys_low = summed[0].astype(jnp.bfloat16)
    values_grad_low = summed[1].astype(jnp.bfloat16)
    queries_low = query_unrotated_gradient.astype(jnp.bfloat16)
    query_weight_grad = inner(normed_full, queries_low)
    key_weight_grad = inner(normed_full, keys_low)
    value_weight_grad = inner(normed_full, values_grad_low)
    normed_grad = spread_sum(against(queries_low, query_projection_weight))
    key_rows = lax.dynamic_slice_in_dim(key_weight, rank * share, share, 0)
    value_rows = lax.dynamic_slice_in_dim(value_weight, rank * share, share, 0)
    normed_grad = normed_grad + against(keys_low, key_rows) + against(values_grad_low, value_rows)
    input_part, attention_gain_grad = norm_backward(inputs, first_rms, attention_gain, normed_grad)
    input_gradient = middle_grad + input_part
    totals = (
        lax.psum(attention_gain_grad.astype(jnp.bfloat16), "dp").astype(jnp.float32),
        lax.psum(query_weight_grad.astype(jnp.bfloat16), "dp").astype(jnp.float32),
        lax.psum(key_weight_grad.astype(jnp.bfloat16), "dp").astype(jnp.float32),
        lax.psum(value_weight_grad.astype(jnp.bfloat16), "dp").astype(jnp.float32),
        lax.psum(summed[2].astype(jnp.bfloat16), "dp").astype(jnp.float32),
        lax.psum(summed[3].astype(jnp.bfloat16), "dp").astype(jnp.float32),
        lax.psum(output_weight_grad.astype(jnp.bfloat16), "dp").astype(jnp.float32),
        lax.psum(feedforward_gain_grad.astype(jnp.bfloat16), "dp").astype(jnp.float32),
        lax.psum(gate_weight_grad.astype(jnp.bfloat16), "dp").astype(jnp.float32),
        lax.psum(up_weight_grad.astype(jnp.bfloat16), "dp").astype(jnp.float32),
        lax.psum(down_grad.astype(jnp.bfloat16), "dp").astype(jnp.float32),
    )
    return (
        output,
        input_gradient,
        totals[0],
        totals[1],
        totals[2],
        totals[3],
        totals[4],
        totals[5],
        totals[6],
        totals[7],
        totals[8],
        totals[9],
        totals[10],
    )


def solution(mesh):
    in_specs = (
        P("dp", "mp"),
        P("dp"),
        P(),
        P("mp"),
        P(None, "mp"),
        P(),
        P(),
        P(),
        P(),
        P(None, "mp"),
        P("mp"),
        P(None, "mp"),
        P(None, "mp"),
        P("mp", None),
        P("dp", "mp"),
    )
    out_specs = (
        P("dp", "mp"),
        P("dp", "mp"),
        P("mp"),
        P(None, "mp"),
        P(),
        P(),
        P(),
        P(),
        P(None, "mp"),
        P("mp"),
        P(None, "mp"),
        P(None, "mp"),
        P("mp", None),
    )
    return jax.shard_map(
        on_device, mesh=mesh, in_specs=in_specs, out_specs=out_specs, check_vma=False
    )
```

profile of v0, /device:TPU:0, one launch (start us, length us, event | category | flops | bytes accessed | tf_op | source)
XLA Modules:
  0.0 2038.4 jit_solution(6352952060460513605)
XLA Ops:
  13.3 13.7 psum.133
  34.5 8.1 fusion.86
  43.9 135.8 %all-gather.5.cloned.1.call-done = bf16[2048,2048]{0,1:T(8,128)(2,1)} async-done(((bf16[2048,512]{0,1:T(8,128)(2,1)}), bf16[2048,2048]{0,1:T(8,128)(2,1)}) %all-gather.5.cloned.1.call-update) | async-done | bytes 8388624 | tf_op jit(solution)/shard_map/all_gather | solution.py:53
  179.8 7.4 convolution_convert_fusion.8
  216.0 6.7 fusion.62
  225.3 5.2 fusion.107
  230.5 5.8 reshape.296
  250.4 6.5 fusion.77
  256.9 5.7 reshape.314
  265.4 75.8 %while.30 = (s32[]{:T(128)}, bf16[2,2,6,512,64]{3,4,2,1,0:T(8,128)(2,1)}, f32[2,2,6,512]{3,2,1,0:T(8,128)S(1)}, s32[2]{0:T(128)S(1)}, bf16[2,2,6,512,64]{3,4,2,1...) while((s32[]{:T(128)}, ...), condition=%wide.region_8.9_spmd.clone.clone, body=%wide.region_5.8_spmd.clone.sunk.clone | while | flops 1686628864 | bytes 190279856 | solution.py:157
  267.4 12.2 fusion.187
  279.6 12.3 fusion.188
  295.0 8.5 bitcast_dynamic-update-slice_fusion.9
  305.2 12.2 fusion.187
  317.4 12.3 fusion.188
  332.7 8.5 bitcast_dynamic-update-slice_fusion.9
  347.0 113.7 %all-gather.7.cloned.1.call-done = bf16[2048,1536]{0,1:T(8,128)(2,1)} async-done(((bf16[2048,384]{0,1:T(8,128)(2,1)}), bf16[2048,1536]{0,1:T(8,128)(2,1)}) %all-gather.7.cloned.1.call-update) | async-done | bytes 6291472 | tf_op jit(solution)/shard_map/all_gather | solution.py:161
  460.7 8.3 multiply_reduce_fusion.1
  469.0 8.8 psum.134
  482.3 148.5 %all-gather.9.cloned.1.call-done = bf16[2048,2048]{0,1:T(8,128)(2,1)} async-done(((bf16[2048,512]{0,1:T(8,128)(2,1)}), bf16[2048,2048]{0,1:T(8,128)(2,1)}) %all-gather.9.cloned.1.call-update) | async-done | bytes 8388624 | tf_op jit(solution)/shard_map/all_gather | solution.py:53
  630.8 14.9 fusion.109
  645.8 11.6 fusion.108
  657.3 122.8 %all-gather.11.cloned.1.call-done = bf16[2048,2048]{1,0:T(8,128)(2,1)} async-done(((bf16[2048,512]{1,0:T(8,128)(2,1)}), bf16[2048,2048]{1,0:T(8,128)(2,1)}) %all-gather.11.cloned.1.call-update) | async-done | bytes 8388624 | tf_op jit(solution)/shard_map/all_gather | solution.py:177
  780.1 23.6 %multiply_convert_fusion.1 = (bf16[2048,1024]{1,0:T(8,128)(2,1)}, bf16[2048,1024]{1,0:T(8,128)(2,1)}, bf16[2048,1024]{1,0:T(8,128)(2,1)}) fusion(f32[2048,1024]{1,0:T(8,128)} %fusion.108, f32[2048,1024]{1,0:T(8,128)} %fusion.109, bf16[2048,2048]{1,0:T(8,128)(2,1)} %all-gather.11.cloned.1.call-done, bf16[1024,2048]{1,0:T(8,128)(2,1)} %param.32), kind=kOutput, calls=%fused_computation.53 | convolution fusion | flops 8621391872 | bytes 41943040 | tf_op jit(solution)/shard_map/dot_general | solution.py:44
  803.8 15.4 fusion.110
  819.2 14.4 add_convert_fusion
  833.6 14.0 convolution_convert_fusion.2
  851.6 124.8 %reduce-scatter.9.cloned.1.call-done = bf16[2048,512]{0,1:T(8,128)(2,1)} async-done(((bf16[2048,2048]{0,1:T(8,128)(2,1)}), bf16[2048,512]{0,1:T(8,128)(2,1)}) %reduce-scatter.9.cloned.1.call-update) | async-done | bytes 2097168 | tf_op jit(solution)/shard_map/reduce_scatter | solution.py:65
  981.1 11.6 psum.135
  992.7 131.9 %reduce-scatter.7.cloned.1.call-done = bf16[2048,512]{0,1:T(8,128)(2,1)} async-done(((bf16[2048,2048]{0,1:T(8,128)(2,1)}), bf16[2048,512]{0,1:T(8,128)(2,1)}) %reduce-scatter.7.cloned.1.call-update) | async-done | bytes 2097168 | tf_op jit(solution)/shard_map/reduce_scatter | solution.py:173
  1124.6 6.0 fusion.39
  1132.6 5.4 convolution_convert_fusion.1
  1138.1 8.6 copy.163
  1150.4 14.7 convolution_convert_fusion.3
  1165.1 12.8 convolution_convert_fusion.4
  1178.0 10.4 convolution_convert_fusion.5
  1193.4 64.9 %reduce-scatter.13.cloned.1.call-done = bf16[384,2048]{1,0:T(8,128)(2,1)} async-done(((bf16[1536,2048]{1,0:T(8,128)(2,1)}), bf16[384,2048]{1,0:T(8,128)(2,1)}) %reduce-scatter.13.cloned.1.call-update) | async-done | bytes 1572880
  1262.3 5.6 reshape.310
  1272.1 5.8 reshape.315
  1280.8 164.1 %while.31 = (s32[]{:T(128)}, f32[2,6,1024,64]{2,3,1,0:T(8,128)}, f32[2,6,1024,64]{2,3,1,0:T(8,128)}, f32[2,2,6,512,64]{3,4,2,1,0:T(8,128)}, s32[2]{0:T(128)S(1)}...) while((s32[]{:T(128)}, f32[2,6,1024,64]{2,3,1,0:T(8,128)}, ...), condition=%wide.region_19.20_spmd.clone.clone, body=%wide.region_17.19_spmd.clone.sunk.clone | while | flops 4125747712 | bytes 278057216 | solution.py:227
  1283.0 11.5 fusion.198
  1294.5 13.4 select_add_fusion.7
  1307.9 18.2 multiply_reduce_fusion.10
  1326.1 17.3 multiply_convert_fusion.8
  1352.0 9.7 bitcast_dynamic-update-slice_fusion.11
  1363.4 11.5 fusion.198
  1374.9 14.3 select_add_fusion.7
  1389.2 18.2 multiply_reduce_fusion.10
  1407.4 17.3 multiply_convert_fusion.8
  1429.2 6.0 select_add_fusion.6
  1435.2 9.7 bitcast_dynamic-update-slice_fusion.11
  1486.0 5.8 convolution_convert_fusion.7
  1491.8 91.7 %all-reduce.13.cloned.1.call-done = (bf16[2048,320]{0,1:T(8,128)(2,1)}, bf16[2048,320]{0,1:T(8,128)(2,1)}) async-done(((bf16[2048,320]{0,1:T(8,128)(2,1)}, bf16[2048,320]{0,1:T(8,128)(2,1)}), (bf16[2048,320]{0,1:T(8,128)(2,1)}, bf16[2048,320]{0,1:T(8,128)(2,1)})) %all-reduce.13.cloned.1.call-update) | async-done | bytes 2621456 | tf_op jit(solution)/shard_map/psum | solution.py:237
  1583.5 7.8 convolution_convert_fusion.10
  1591.3 7.4 convolution_convert_fusion.9
  1600.1 6.7 convolution_convert_fusion
  1611.0 10.2 all-reduce.6
  1625.4 210.8 %all-reduce.11.cloned.1.call-done = (bf16[2048,384]{1,0:T(8,128)(2,1)}, bf16[2048,320]{0,1:T(8,128)(2,1)}, bf16[2048,320]{0,1:T(8,128)(2,1)}, bf16[1536,512]{1,0...) async-done(((bf16[2048,384]{1,0:T(8,128)(2,1)}, bf16[2048,320]{0,1:T(8,128)(2,1)}, bf16[2048,320]{0,1:T(8,128)(2,1)}, ...) | async-done | bytes 18350096 | tf_op jit(solution)/shard_map/psum | solution.py:256
  1860.1 122.8 %reduce-scatter.11.cloned.1.call-done = bf16[2048,512]{0,1:T(8,128)(2,1)} async-done(((bf16[2048,2048]{0,1:T(8,128)(2,1)}), bf16[2048,512]{0,1:T(8,128)(2,1)}) %reduce-scatter.11.cloned.1.call-update) | async-done | bytes 2097168 | tf_op jit(solution)/shard_map/reduce_scatter | solution.py:65
  1982.9 7.8 fusion.52
  1990.7 13.5 all-reduce.4
  2006.3 11.7 psum.138
  2018.1 7.7 fusion.49
  2025.8 5.3 copy.146
  (300 shorter events, 206.1 us)
Async XLA Ops:
  7.2 218.1 %copy-start = (bf16[2048,384]{1,0:T(8,128)(2,1)S(1)}, bf16[2048,384]{1,0:T(8,128)(2,1)}, u32[]{:S(2)}) copy-start(bf16[2048,384]{1,0:T(8,128)(2,1)} %param.23) | copy-start | bytes 4718596
  7.2 21.1 %copy-start.48 = (f32[512]{0:T(512)S(1)}, f32[512]{0:T(512)}, u32[]{:S(2)}) copy-start(f32[512]{0:T(512)} %param.22) | copy-start | bytes 6148
  7.2 172.6 %all-gather.5.cloned.1.call-start = ((), (), s32[]{:S(2)}) async-start(), calls=%async_computation.4 | async-start | bytes 10485760 | tf_op jit(solution)/shard_map/all_gather | solution.py:53
  28.3 3.5 copy-start.52
  28.3 3.6 copy-start.61
  31.7 148.1 %copy-start.43 = (bf16[2048,320]{0,1:T(8,128)(2,1)S(1)}, bf16[2048,320]{0,1:T(8,128)(2,1)}, u32[]{:S(2)}) copy-start(bf16[2048,320]{0,1:T(8,128)(2,1)} %param.25) | copy-start | bytes 3932164
  31.7 429.0 %all-gather.7.cloned.1.call-start = ((), (), s32[]{:S(2)}) async-start(), calls=%async_computation.5 | async-start | bytes 7864320 | tf_op jit(solution)/shard_map/all_gather | solution.py:161
  31.9 155.3 %copy-start.58 = (f32[32]{0:T(128)}, f32[32]{0:T(128)S(1)}, u32[]{:S(2)}) copy-start(f32[32]{0:T(128)S(1)} %multiply_exponential_fusion) | copy-start | bytes 388
  33.2 189.5 %copy-start.50 = (s32[6]{0:T(128)}, s32[6]{0:T(128)S(1)}, u32[]{:S(2)}) copy-start(s32[6]{0:T(128)S(1)} %fusion.101) | copy-start | bytes 76
  42.6 173.4 %copy-start.16 = (f32[2,1024,64]{1,0,2:T(2,128)}, f32[2,1024,64]{1,0,2:T(2,128)S(1)}, u32[]{:S(2)}) copy-start(f32[2,1024,64]{1,0,2:T(2,128)S(1)} %get-tuple-element.371) | copy-start | bytes 1572868
  190.7 3.7 copy-start.63
  199.6 7.5 copy-start.53
  216.0 9.3 slice-start
  267.4 24.5 %copy-start.9 = (bf16[2,6,1024,64]{2,3,1,0:T(8,128)(2,1)S(1)}, bf16[2,6,1024,64]{2,3,1,0:T(8,128)(2,1)}, u32[]{:S(2)}) copy-start(bf16[2,6,1024,64]{2,3,1,0:T(8,128)(2,1)} %get-tuple-element.557) | copy-start | bytes 4718596 | tf_op jit(solution)/shard_map/while
  279.6 15.4 copy-start.2
  305.2 24.5 %copy-start.9 = (bf16[2,6,1024,64]{2,3,1,0:T(8,128)(2,1)S(1)}, bf16[2,6,1024,64]{2,3,1,0:T(8,128)(2,1)}, u32[]{:S(2)}) copy-start(bf16[2,6,1024,64]{2,3,1,0:T(8,128)(2,1)} %get-tuple-element.557) | copy-start | bytes 4718596 | tf_op jit(solution)/shard_map/while
  317.4 15.4 copy-start.2
  345.3 115.4 %copy-start.67 = (bf16[1536,512]{1,0:T(8,128)(2,1)S(1)}, bf16[1536,512]{1,0:T(8,128)(2,1)}, u32[]{:S(2)}) copy-start(bf16[1536,512]{1,0:T(8,128)(2,1)} %param.28) | copy-start | bytes 4718596
  347.0 130.8 %copy-start.47 = (f32[512]{0:T(512)S(1)}, f32[512]{0:T(512)}, u32[]{:S(2)}) copy-start(f32[512]{0:T(512)} %param.29) | copy-start | bytes 6148
  347.0 283.8 %all-gather.9.cloned.1.call-start = ((), (), s32[]{:S(2)}) async-start(), calls=%async_computation.6 | async-start | bytes 10485760 | tf_op jit(solution)/shard_map/all_gather | solution.py:53
  481.7 298.4 %all-gather.11.cloned.1.call-start = ((), (), s32[]{:S(2)}) async-start(), calls=%async_computation.8 | async-start | bytes 10485760 | tf_op jit(solution)/shard_map/all_gather | solution.py:177
  482.3 494.1 %reduce-scatter.9.cloned.1.call-start = ((), (), s32[]{:S(2)}) async-start(), calls=%async_computation.9 | async-start | bytes 10485760 | tf_op jit(solution)/shard_map/reduce_scatter | solution.py:65
  630.8 14.9 copy-start.64
  630.8 14.9 copy-start.65
  803.8 15.4 copy-start.66
  803.8 15.4 copy-start.70
  833.6 291.0 %reduce-scatter.7.cloned.1.call-start = ((), (), s32[]{:S(2)}) async-start(), calls=%async_computation.7 | async-start | bytes 10485760 | tf_op jit(solution)/shard_map/reduce_scatter | solution.py:173
  847.7 410.7 %reduce-scatter.13.cloned.1.call-start = ((), (), s32[]{:S(2)}) async-start(), calls=%async_computation.11 | async-start | bytes 7864320
  1146.7 436.8 %all-reduce.13.cloned.1.call-start = ((), (), s32[]{:S(2)}) async-start(), calls=%async_computation.13 | async-start | bytes 5242880 | tf_op jit(solution)/shard_map/psum | solution.py:237
  1150.4 14.7 copy-start.71
  1150.4 27.5 %slice-start.4 = ((s8[8388608]{0:T(1024)(128)(4,1)}), s8[4194304]{0:T(1024)(128)(4,1)S(1)}, s32[]{:S(2)}) async-start(s8[8388608]{0:T(1024)(128)(4,1)} %bitcast.239), calls=%async_computation.18 | async-start | bytes 8388608
  1165.1 12.9 slice-start.5
  1165.1 12.9 copy-start.72
  1165.1 23.3 %slice-start.6 = ((s8[6291456]{0:T(1024)(128)(4,1)}), s8[4194304]{0:T(1024)(128)(4,1)S(1)}, s32[]{:S(2)}) async-start(s8[6291456]{0:T(1024)(128)(4,1)} %bitcast.241), calls=%async_computation.20 | async-start | bytes 8388608
  1177.9 10.4 copy-start.15
  1178.0 10.4 slice-start.7
  1262.3 5.6 copy-start.60
  1272.1 8.7 copy-start.4
  1272.1 8.7 copy-start.39
  1272.1 8.7 copy-start.69
  1283.0 11.5 copy-start.5
  1283.0 11.5 copy-start.13
  1326.1 21.8 %copy-start.6 = (bf16[2,2,6,512,64]{3,4,2,1,0:T(8,128)(2,1)S(1)}, bf16[2,2,6,512,64]{3,4,2,1,0:T(8,128)(2,1)}, u32[]{:S(2)}) copy-start(bf16[2,2,6,512,64]{3,4,2,1,0:T(8,128)(2,1)} %get-tuple-element.583) | copy-start | bytes 4718596 | tf_op jit(solution)/shard_map/while
  1343.5 4.5 copy-start.1
  1363.4 11.5 copy-start.5
  1363.4 11.5 copy-start.13
  1407.4 21.8 %copy-start.6 = (bf16[2,2,6,512,64]{3,4,2,1,0:T(8,128)(2,1)S(1)}, bf16[2,2,6,512,64]{3,4,2,1,0:T(8,128)(2,1)}, u32[]{:S(2)}) copy-start(bf16[2,2,6,512,64]{3,4,2,1,0:T(8,128)(2,1)} %get-tuple-element.583) | copy-start | bytes 4718596 | tf_op jit(solution)/shard_map/while
  1424.8 4.5 copy-start.1
  1463.1 4.9 copy-start.18
  1478.3 357.9 %all-reduce.11.cloned.1.call-start = ((), (), s32[]{:S(2)}) async-start(), calls=%async_computation.12 | async-start | bytes 36700160 | tf_op jit(solution)/shard_map/psum | solution.py:256
  1478.4 3.8 copy-start.11
  1478.4 7.6 slice-start.2
  1482.2 3.8 slice-start.3
  1583.5 7.8 copy-start.32
  1598.8 384.1 %reduce-scatter.11.cloned.1.call-start = ((), (), s32[]{:S(2)}) async-start(), calls=%async_computation.10 | async-start | bytes 10485760 | tf_op jit(solution)/shard_map/reduce_scatter | solution.py:65
  1606.9 14.2 copy-start.22
  1839.6 3.6 copy-start.27
  1846.7 4.4 copy-start.20
  1851.2 4.4 copy-start.19
  1855.6 127.3 %copy-start.33 = (bf16[2048,320]{0,1:T(8,128)(2,1)S(1)}, bf16[2048,320]{0,1:T(8,128)(2,1)}, u32[]{:S(2)}) copy-start(bf16[2048,320]{0,1:T(8,128)(2,1)} %get-tuple-element.349) | copy-start | bytes 3932164
  1855.6 127.3 %copy-start.41 = (f32[2048]{0:T(1024)S(1)}, f32[2048]{0:T(1024)}, u32[]{:S(2)}) copy-start(f32[2048]{0:T(1024)} %copy-done.40) | copy-start | bytes 24580
  1855.6 127.3 %copy-start.49 = (f32[512]{0:T(512)S(1)}, f32[512]{0:T(512)}, u32[]{:S(2)}) copy-start(f32[512]{0:T(512)} %param.22) | copy-start | bytes 6148
  1860.1 130.7 %copy-start.57 = (bf16[512]{0:T(512)(128)(2,1)S(1)}, bf16[512]{0:T(512)(128)(2,1)}, u32[]{:S(2)}) copy-start(bf16[512]{0:T(512)(128)(2,1)} %get-tuple-element.291) | copy-start | bytes 3076
  1860.1 158.0 %copy-start.46 = (f32[2048]{0:T(1024)S(1)}, f32[2048]{0:T(1024)}, u32[]{:S(2)}) copy-start(f32[2048]{0:T(1024)} %get-tuple-element.373) | copy-start | bytes 24580
  (33 other events, 66.4 us)
Sparse Core Ops, SparseCore 0:
  31.9 147.8 all-gather.4
  347.1 113.5 all-gather.6
  481.8 148.9 all-gather.8
  632.2 147.8 all-gather.10
  833.7 142.6 reduce-scatter.8
  979.2 145.3 reduce-scatter.6
  1146.8 111.4 reduce-scatter.12
  1478.4 105.0 all-reduce.12
  1598.9 237.2 all-reduce.10
  1838.4 144.4 reduce-scatter.10
where the time goes:
time: 2050 us; the launch traced here: 2040 us
  waiting for transfers between devices  1270 us (62%)
  matrix products  376 us (18%)
  other arithmetic  173 us (8%)
  local copies, waits for them, and re-layouts  134 us (7%)
  blocking collectives  69.5 us (3%)
    all_gather x2, waiting for transfers between devices, norm_forward(): return (rms, lax.all_gather(normed, 'mp', axis=1, tiled=True))  284 us
    reduce_scatter x2, waiting for transfers between devices, spread_sum(): lax.psum_scatter(terms.astype(jnp.bfloat16), 'mp', scatter_dimension=1, t...  248 us
    psum x1, waiting for transfers between devices, on_device(): lax.psum(query_weight_grad.astype(jnp.bfloat16), 'dp').astype(jnp.float32)  211 us
    reduce_scatter x1, waiting for transfers between devices, on_device(): lax.psum_scatter(down_terms.astype(jnp.bfloat16), 'mp', scatter_dimension...  132 us
    all_gather x1, waiting for transfers between devices, on_device(): cotangent_full = lax.all_gather(cotangent, 'mp', axis=1, tiled=True)  123 us
    all_gather x1, waiting for transfers between devices, on_device(): all_heads = lax.all_gather(mixed_local, 'mp', axis=1, tiled=True)  114 us
    psum x1, waiting for transfers between devices, on_device(): lax.psum(key_raw_grad.astype(jnp.bfloat16), 'mp').astype(jnp.float32)  91.7 us
    dot_general x7, matrix products, against(): lax.dot_general(left_operand, right_operand, (((1,), (1,)), ((), ())), pr...  77.7 us
  transfers between devices with their start and end apart: 10, of which 10 were waited for; matrix products, arithmetic and copies ran while one was open for 8% of the time, Pallas kernels for 0%

commit v1 on v0

--- a/solution.py
+++ b/solution.py
@@ -234,7 +234,9 @@
     query_unrotated_gradient, query_gain_part = query_pull(query_rot_grad)
     key_raw_grad, key_gain_part = key_pull(key_rot_grad)
     summed = (
-        lax.psum(key_raw_grad.astype(jnp.bfloat16), "mp").astype(jnp.float32),
+        jnp.sum(lax.all_gather(key_raw_grad.astype(jnp.bfloat16), "mp"), axis=0).astype(
+            jnp.float32
+        ),
         lax.psum(value_grad.astype(jnp.bfloat16), "mp").astype(jnp.float32),
         lax.psum(query_gain_part.astype(jnp.bfloat16), "mp").astype(jnp.float32),
         lax.psum(key_gain_part.astype(jnp.bfloat16), "mp").astype(jnp.float32),

time: 2050 us -> 2050 us (level)
    psum x1, waiting for transfers between devices: 91.7 us -> 0.01 us  [on_device(): lax.psum(value_grad.astype(jnp.bfloat16), 'mp').astype(jnp.float32)]
    all_gather x0 -> x1, waiting for transfers between devices: none -> 67.5 us  [on_device(): lax.all_gather(key_raw_grad.astype(jnp.bfloat16), 'mp')]
    unnamed x11 -> x12, waiting for transfers between devices: 65.6 us -> 109 us
    unnamed x162 -> x146, local copies, waits for them, and re-layouts: 52.8 us -> 49.7 us
  transfers between devices with their start and end apart: 10 -> 11, of which waited for: 10 -> 10; matrix products, arithmetic and copies ran while one was open for 8% -> 10% of each run, Pallas kernels for 0% -> 0%
where the time goes in v1:
time: 2050 us; the launch traced here: 2030 us
  waiting for transfers between devices  1270 us (62%)
  matrix products  378 us (18%)
  other arithmetic  174 us (8%)
  local copies, waits for them, and re-layouts  129 us (6%)
  blocking collectives  69.4 us (3%)
    all_gather x2, waiting for transfers between devices, norm_forward(): return (rms, lax.all_gather(normed, 'mp', axis=1, tiled=True))  284 us
    reduce_scatter x2, waiting for transfers between devices, spread_sum(): lax.psum_scatter(terms.astype(jnp.bfloat16), 'mp', scatter_dimension=1, t...  242 us
    psum x1, waiting for transfers between devices, on_device(): lax.psum(query_weight_grad.astype(jnp.bfloat16), 'dp').astype(jnp.float32)  196 us
    reduce_scatter x1, waiting for transfers between devices, on_device(): lax.psum_scatter(down_terms.astype(jnp.bfloat16), 'mp', scatter_dimension...  132 us
    all_gather x1, waiting for transfers between devices, on_device(): cotangent_full = lax.all_gather(cotangent, 'mp', axis=1, tiled=True)  123 us
    all_gather x1, waiting for transfers between devices, on_device(): all_heads = lax.all_gather(mixed_local, 'mp', axis=1, tiled=True)  114 us
    unnamed x12, waiting for transfers between devices  109 us
    dot_general x7, matrix products, against(): lax.dot_general(left_operand, right_operand, (((1,), (1,)), ((), ())), pr...  78.1 us
  transfers between devices with their start and end apart: 11, of which 10 were waited for; matrix products, arithmetic and copies ran while one was open for 10% of the time, Pallas kernels for 0%

profile of v1, /device:TPU:0, one launch (start us, length us, event | category | flops | bytes accessed | tf_op | source)
XLA Modules:
  0.0 2034.2 jit_solution(8335228176183180837)
XLA Ops:
  13.4 13.7 psum.126
  34.5 8.1 fusion.86
  44.0 135.8 %all-gather.6.cloned.1.call-done = bf16[2048,2048]{0,1:T(8,128)(2,1)} async-done(((bf16[2048,512]{0,1:T(8,128)(2,1)}), bf16[2048,2048]{0,1:T(8,128)(2,1)}) %all-gather.6.cloned.1.call-update) | async-done | bytes 8388624 | tf_op jit(solution)/shard_map/all_gather | solution.py:53
  179.8 7.3 convolution_convert_fusion.8
  216.0 6.7 fusion.62
  225.3 5.2 fusion.107
  230.4 5.8 reshape.306
  250.3 6.5 fusion.77
  256.8 5.7 reshape.324
  265.4 75.7 %while.30 = (s32[]{:T(128)}, bf16[2,2,6,512,64]{3,4,2,1,0:T(8,128)(2,1)}, f32[2,2,6,512]{3,2,1,0:T(8,128)S(1)}, s32[2]{0:T(128)S(1)}, bf16[2,2,6,512,64]{3,4,2,1...) while((s32[]{:T(128)}, ...), condition=%wide.region_8.9_spmd.clone.clone, body=%wide.region_5.8_spmd.clone.sunk.clone | while | flops 1686628864 | bytes 190279856 | solution.py:157
  267.4 12.1 fusion.187
  279.5 12.3 fusion.188
  294.9 8.5 bitcast_dynamic-update-slice_fusion.9
  305.0 12.1 fusion.187
  317.1 12.3 fusion.188
  332.5 8.5 bitcast_dynamic-update-slice_fusion.9
  346.8 113.7 %all-gather.8.cloned.1.call-done = bf16[2048,1536]{0,1:T(8,128)(2,1)} async-done(((bf16[2048,384]{0,1:T(8,128)(2,1)}), bf16[2048,1536]{0,1:T(8,128)(2,1)}) %all-gather.8.cloned.1.call-update) | async-done | bytes 6291472 | tf_op jit(solution)/shard_map/all_gather | solution.py:161
  460.5 8.3 multiply_reduce_fusion.1
  468.8 8.8 psum.127
  482.1 148.5 %all-gather.10.cloned.1.call-done = bf16[2048,2048]{0,1:T(8,128)(2,1)} async-done(((bf16[2048,512]{0,1:T(8,128)(2,1)}), bf16[2048,2048]{0,1:T(8,128)(2,1)}) %all-gather.10.cloned.1.call-update) | async-done | bytes 8388624 | tf_op jit(solution)/shard_map/all_gather | solution.py:53
  630.6 14.9 fusion.109
  645.5 11.6 fusion.108
  657.1 122.8 %all-gather.12.cloned.1.call-done = bf16[2048,2048]{1,0:T(8,128)(2,1)} async-done(((bf16[2048,512]{1,0:T(8,128)(2,1)}), bf16[2048,2048]{1,0:T(8,128)(2,1)}) %all-gather.12.cloned.1.call-update) | async-done | bytes 8388624 | tf_op jit(solution)/shard_map/all_gather | solution.py:177
  779.9 23.7 %multiply_convert_fusion.1 = (bf16[2048,1024]{1,0:T(8,128)(2,1)}, bf16[2048,1024]{1,0:T(8,128)(2,1)}, bf16[2048,1024]{1,0:T(8,128)(2,1)}) fusion(f32[2048,1024]{1,0:T(8,128)} %fusion.108, f32[2048,1024]{1,0:T(8,128)} %fusion.109, bf16[2048,2048]{1,0:T(8,128)(2,1)} %all-gather.12.cloned.1.call-done, bf16[1024,2048]{1,0:T(8,128)(2,1)} %param.32), kind=kOutput, calls=%fused_computation.53 | convolution fusion | flops 8621391872 | bytes 41943040 | tf_op jit(solution)/shard_map/dot_general | solution.py:44
  803.7 15.3 fusion.110
  819.0 14.4 add_convert_fusion
  833.4 14.0 convolution_convert_fusion.2
  851.4 124.8 %reduce-scatter.9.cloned.1.call-done = bf16[2048,512]{0,1:T(8,128)(2,1)} async-done(((bf16[2048,2048]{0,1:T(8,128)(2,1)}), bf16[2048,512]{0,1:T(8,128)(2,1)}) %reduce-scatter.9.cloned.1.call-update) | async-done | bytes 2097168 | tf_op jit(solution)/shard_map/reduce_scatter | solution.py:65
  980.9 11.7 psum.128
  992.5 131.9 %reduce-scatter.7.cloned.1.call-done = bf16[2048,512]{0,1:T(8,128)(2,1)} async-done(((bf16[2048,2048]{0,1:T(8,128)(2,1)}), bf16[2048,512]{0,1:T(8,128)(2,1)}) %reduce-scatter.7.cloned.1.call-update) | async-done | bytes 2097168 | tf_op jit(solution)/shard_map/reduce_scatter | solution.py:173
  1124.4 6.1 fusion.39
  1132.5 5.4 convolution_convert_fusion.1
  1137.9 8.6 copy.163
  1150.0 108.2 %reduce-scatter.13.cloned.1.call-done = bf16[384,2048]{1,0:T(8,128)(2,1)} async-done(((bf16[1536,2048]{1,0:T(8,128)(2,1)}), bf16[384,2048]{1,0:T(8,128)(2,1)}) %reduce-scatter.13.cloned.1.call-update) | async-done | bytes 1572880
  1262.2 5.6 reshape.320
  1272.0 5.8 reshape.325
  1280.7 164.2 %while.31 = (s32[]{:T(128)}, f32[2,6,1024,64]{2,3,1,0:T(8,128)}, f32[2,6,1024,64]{2,3,1,0:T(8,128)}, f32[2,2,6,512,64]{3,4,2,1,0:T(8,128)}, s32[2]{0:T(128)S(1)}...) while((s32[]{:T(128)}, f32[2,6,1024,64]{2,3,1,0:T(8,128)}, ...), condition=%wide.region_19.20_spmd.clone.clone, body=%wide.region_17.19_spmd.clone.sunk.clone | while | flops 4125747712 | bytes 278057216 | solution.py:227
  1282.6 11.6 fusion.198
  1294.2 13.4 select_add_fusion.7
  1307.6 18.2 multiply_reduce_fusion.10
  1325.7 17.3 multiply_convert_fusion.8
  1351.7 9.7 bitcast_dynamic-update-slice_fusion.11
  1363.0 11.6 fusion.198
  1374.6 14.3 select_add_fusion.7
  1388.9 18.2 multiply_reduce_fusion.10
  1407.0 17.3 multiply_convert_fusion.8
  1428.9 6.0 select_add_fusion.6
  1434.9 9.7 bitcast_dynamic-update-slice_fusion.11
  1479.4 6.7 convolution_convert_fusion
  1486.3 14.7 convolution_convert_fusion.3
  1501.0 12.8 convolution_convert_fusion.4
  1513.8 12.5 convolution_convert_fusion.5
  1531.4 5.6 convolution_convert_fusion.7
  1537.1 7.8 convolution_convert_fusion.9
  1544.8 67.5 %all-gather.14.cloned.1.call-done = bf16[4,2048,320]{1,2,0:T(8,128)(2,1)} async-done(((bf16[1,2048,320]{1,2,0:T(8,128)(2,1)}), bf16[4,2048,320]{1,2,0:T(8,128)(2,1)}) %all-gather.14.cloned.1.call-update) | async-done | bytes 5242896 | tf_op jit(solution)/shard_map/all_gather | solution.py:237
  1615.9 7.3 convolution_convert_fusion.10
  1627.2 9.7 all-reduce.6
  1641.2 116.9 %reduce-scatter.11.cloned.1.call-done = bf16[2048,512]{0,1:T(8,128)(2,1)} async-done(((bf16[2048,2048]{0,1:T(8,128)(2,1)}), bf16[2048,512]{0,1:T(8,128)(2,1)}) %reduce-scatter.11.cloned.1.call-update) | async-done | bytes 2097168 | tf_op jit(solution)/shard_map/reduce_scatter | solution.py:65
  1758.2 8.2 fusion.52
  1766.4 13.8 all-reduce.4
  1782.3 11.8 psum.130
  1794.1 8.4 fusion.49
  1802.5 5.3 copy.146
  1807.8 195.9 %all-reduce.12.cloned.1.call-done = (bf16[2048,384]{1,0:T(8,128)(2,1)}, bf16[2048,320]{0,1:T(8,128)(2,1)}, bf16[2048,320]{0,1:T(8,128)(2,1)}, bf16[1536,512]{1,0...) async-done(((bf16[2048,384]{1,0:T(8,128)(2,1)}, bf16[2048,320]{0,1:T(8,128)(2,1)}, bf16[2048,320]{0,1:T(8,128)(2,1)}, ...) | async-done | bytes 18350096 | tf_op jit(solution)/shard_map/psum | solution.py:258
  (288 shorter events, 201.6 us)
Async XLA Ops:
  7.2 218.0 %copy-start = (bf16[2048,384]{1,0:T(8,128)(2,1)S(1)}, bf16[2048,384]{1,0:T(8,128)(2,1)}, u32[]{:S(2)}) copy-start(bf16[2048,384]{1,0:T(8,128)(2,1)} %param.23) | copy-start | bytes 4718596
  7.2 21.1 %copy-start.41 = (f32[512]{0:T(512)S(1)}, f32[512]{0:T(512)}, u32[]{:S(2)}) copy-start(f32[512]{0:T(512)} %param.22) | copy-start | bytes 6148
  7.2 172.6 %all-gather.6.cloned.1.call-start = ((), (), s32[]{:S(2)}) async-start(), calls=%async_computation.4 | async-start | bytes 10485760 | tf_op jit(solution)/shard_map/all_gather | solution.py:53
  28.3 3.5 copy-start.45
  28.3 3.6 copy-start.54
  31.7 148.1 %copy-start.36 = (bf16[2048,320]{0,1:T(8,128)(2,1)S(1)}, bf16[2048,320]{0,1:T(8,128)(2,1)}, u32[]{:S(2)}) copy-start(bf16[2048,320]{0,1:T(8,128)(2,1)} %param.25) | copy-start | bytes 3932164
  31.7 428.8 %all-gather.8.cloned.1.call-start = ((), (), s32[]{:S(2)}) async-start(), calls=%async_computation.5 | async-start | bytes 7864320 | tf_op jit(solution)/shard_map/all_gather | solution.py:161
  31.9 155.2 %copy-start.51 = (f32[32]{0:T(128)}, f32[32]{0:T(128)S(1)}, u32[]{:S(2)}) copy-start(f32[32]{0:T(128)S(1)} %multiply_exponential_fusion) | copy-start | bytes 388
  33.2 189.4 %copy-start.43 = (s32[6]{0:T(128)}, s32[6]{0:T(128)S(1)}, u32[]{:S(2)}) copy-start(s32[6]{0:T(128)S(1)} %fusion.101) | copy-start | bytes 76
  42.6 173.3 %copy-start.14 = (f32[2,1024,64]{1,0,2:T(2,128)}, f32[2,1024,64]{1,0,2:T(2,128)S(1)}, u32[]{:S(2)}) copy-start(f32[2,1024,64]{1,0,2:T(2,128)S(1)} %get-tuple-element.369) | copy-start | bytes 1572868
  190.7 3.7 copy-start.56
  199.5 7.5 copy-start.46
  216.0 9.3 slice-start
  236.2 3.0 copy-start.48
  267.4 24.4 %copy-start.9 = (bf16[2,6,1024,64]{2,3,1,0:T(8,128)(2,1)S(1)}, bf16[2,6,1024,64]{2,3,1,0:T(8,128)(2,1)}, u32[]{:S(2)}) copy-start(bf16[2,6,1024,64]{2,3,1,0:T(8,128)(2,1)} %get-tuple-element.555) | copy-start | bytes 4718596 | tf_op jit(solution)/shard_map/while
  279.5 15.4 copy-start.2
  305.0 24.4 %copy-start.9 = (bf16[2,6,1024,64]{2,3,1,0:T(8,128)(2,1)S(1)}, bf16[2,6,1024,64]{2,3,1,0:T(8,128)(2,1)}, u32[]{:S(2)}) copy-start(bf16[2,6,1024,64]{2,3,1,0:T(8,128)(2,1)} %get-tuple-element.555) | copy-start | bytes 4718596 | tf_op jit(solution)/shard_map/while
  317.1 15.4 copy-start.2
  345.1 115.4 %copy-start.60 = (bf16[1536,512]{1,0:T(8,128)(2,1)S(1)}, bf16[1536,512]{1,0:T(8,128)(2,1)}, u32[]{:S(2)}) copy-start(bf16[1536,512]{1,0:T(8,128)(2,1)} %param.28) | copy-start | bytes 4718596
  346.8 130.8 %copy-start.40 = (f32[512]{0:T(512)S(1)}, f32[512]{0:T(512)}, u32[]{:S(2)}) copy-start(f32[512]{0:T(512)} %param.29) | copy-start | bytes 6148
  346.8 283.8 %all-gather.10.cloned.1.call-start = ((), (), s32[]{:S(2)}) async-start(), calls=%async_computation.6 | async-start | bytes 10485760 | tf_op jit(solution)/shard_map/all_gather | solution.py:53
  481.5 298.4 %all-gather.12.cloned.1.call-start = ((), (), s32[]{:S(2)}) async-start(), calls=%async_computation.8 | async-start | bytes 10485760 | tf_op jit(solution)/shard_map/all_gather | solution.py:177
  482.1 494.1 %reduce-scatter.9.cloned.1.call-start = ((), (), s32[]{:S(2)}) async-start(), calls=%async_computation.9 | async-start | bytes 10485760 | tf_op jit(solution)/shard_map/reduce_scatter | solution.py:65
  630.6 14.9 copy-start.57
  630.6 14.9 copy-start.58
  803.7 15.3 copy-start.59
  803.7 15.3 copy-start.63
  833.4 291.0 %reduce-scatter.7.cloned.1.call-start = ((), (), s32[]{:S(2)}) async-start(), calls=%async_computation.7 | async-start | bytes 10485760 | tf_op jit(solution)/shard_map/reduce_scatter | solution.py:173
  847.4 410.8 %reduce-scatter.13.cloned.1.call-start = ((), (), s32[]{:S(2)}) async-start(), calls=%async_computation.13 | async-start | bytes 7864320
  1146.6 390.5 %all-reduce.10.cloned.1.call-start = ((), (), s32[]{:S(2)}) async-start(), calls=%async_computation.12 | async-start | bytes 2621440 | tf_op jit(solution)/shard_map/psum | solution.py:240
  1262.2 5.6 copy-start.53
  1272.0 8.7 copy-start.4
  1272.0 8.7 copy-start.32
  1272.0 8.7 copy-start.62
  1280.7 164.3 %copy-start.44 = (s32[6]{0:T(128)S(1)}, s32[6]{0:T(128)}, u32[]{:S(2)}) copy-start(s32[6]{0:T(128)} %copy-done.43) | copy-start | bytes 76
  1282.6 11.6 copy-start.5
  1282.6 11.6 copy-start.11
  1325.7 21.9 %copy-start.6 = (bf16[2,2,6,512,64]{3,4,2,1,0:T(8,128)(2,1)S(1)}, bf16[2,2,6,512,64]{3,4,2,1,0:T(8,128)(2,1)}, u32[]{:S(2)}) copy-start(bf16[2,2,6,512,64]{3,4,2,1,0:T(8,128)(2,1)} %get-tuple-element.581) | copy-start | bytes 4718596 | tf_op jit(solution)/shard_map/while
  1343.0 4.6 copy-start.1
  1363.0 11.6 copy-start.5
  1363.0 11.6 copy-start.11
  1407.0 21.9 %copy-start.6 = (bf16[2,2,6,512,64]{3,4,2,1,0:T(8,128)(2,1)S(1)}, bf16[2,2,6,512,64]{3,4,2,1,0:T(8,128)(2,1)}, u32[]{:S(2)}) copy-start(bf16[2,2,6,512,64]{3,4,2,1,0:T(8,128)(2,1)} %get-tuple-element.581) | copy-start | bytes 4718596 | tf_op jit(solution)/shard_map/while
  1424.4 4.6 copy-start.1
  1451.7 160.6 %all-gather.14.cloned.1.call-start = ((), (), s32[]{:S(2)}) async-start(), calls=%async_computation.11 | async-start | bytes 6553600 | tf_op jit(solution)/shard_map/all_gather | solution.py:237
  1459.0 5.0 copy-start.16
  1472.0 286.2 %reduce-scatter.11.cloned.1.call-start = ((), (), s32[]{:S(2)}) async-start(), calls=%async_computation.10 | async-start | bytes 10485760 | tf_op jit(solution)/shard_map/reduce_scatter | solution.py:65
  1486.2 517.6 %all-reduce.12.cloned.1.call-start = ((), (), s32[]{:S(2)}) async-start(), calls=%async_computation.14 | async-start | bytes 36700160 | tf_op jit(solution)/shard_map/psum | solution.py:258
  1486.3 14.7 copy-start.64
  1486.3 27.5 %slice-start.4 = ((s8[8388608]{0:T(1024)(128)(4,1)}), s8[4194304]{0:T(1024)(128)(4,1)S(1)}, s32[]{:S(2)}) async-start(s8[8388608]{0:T(1024)(128)(4,1)} %bitcast.239), calls=%async_computation.19 | async-start | bytes 8388608
  1501.0 12.8 slice-start.5
  1501.0 25.3 %slice-start.6 = ((s8[6291456]{0:T(1024)(128)(4,1)}), s8[4194304]{0:T(1024)(128)(4,1)S(1)}, s32[]{:S(2)}) async-start(s8[6291456]{0:T(1024)(128)(4,1)} %bitcast.241), calls=%async_computation.21 | async-start | bytes 8388608
  1501.0 30.5 %slice-start.2 = ((s8[8388608]{0:T(1024)(128)(4,1)}), s8[4194304]{0:T(1024)(128)(4,1)S(1)}, s32[]{:S(2)}) async-start(s8[8388608]{0:T(1024)(128)(4,1)} %bitcast.237), calls=%async_computation.17 | async-start | bytes 8388608
  1513.8 12.5 copy-start.13
  1513.8 12.5 slice-start.7
  1513.8 17.6 slice-start.3
  1636.9 121.2 %copy-start.34 = (f32[2048]{0:T(1024)S(1)}, f32[2048]{0:T(1024)}, u32[]{:S(2)}) copy-start(f32[2048]{0:T(1024)} %copy-done.33) | copy-start | bytes 24580
  1636.9 121.2 %copy-start.42 = (f32[512]{0:T(512)S(1)}, f32[512]{0:T(512)}, u32[]{:S(2)}) copy-start(f32[512]{0:T(512)} %param.22) | copy-start | bytes 6148
  1641.2 125.1 %copy-start.50 = (bf16[512]{0:T(512)(128)(2,1)S(1)}, bf16[512]{0:T(512)(128)(2,1)}, u32[]{:S(2)}) copy-start(bf16[512]{0:T(512)(128)(2,1)} %get-tuple-element.291) | copy-start | bytes 3076
  1641.2 152.9 %copy-start.39 = (f32[2048]{0:T(1024)S(1)}, f32[2048]{0:T(1024)}, u32[]{:S(2)}) copy-start(f32[2048]{0:T(1024)} %get-tuple-element.371) | copy-start | bytes 24580
  2003.8 3.4 copy-start.26
  2007.2 3.6 copy-start.24
  2010.8 3.3 copy-start.19
  2014.1 4.4 copy-start.18
  2018.5 4.4 copy-start.17
  (26 other events, 48.0 us)
Sparse Core Ops, SparseCore 0:
  31.9 147.8 all-gather.5
  346.9 113.5 all-gather.7
  481.6 148.9 all-gather.9
  632.0 147.8 all-gather.11
  833.5 142.6 reduce-scatter.8
  979.0 145.3 reduce-scatter.6
  1146.7 111.4 reduce-scatter.12
  1451.8 60.5 all-reduce.9
  1514.5 97.7 all-gather.13
  1615.1 143.0 reduce-scatter.10
  1764.6 239.1 all-reduce.11
